TPU v7x, 1024 devices: a whole 8x8x8 slice. The times are simulated.
1024 devices in a mesh: region: 32 (over y, x_hi, core), member: 32 (over x_lo, z).
Axes of the slice: x: 8 (x_hi: 2, x_lo: 4; x = x_hi * 4 + x_lo), y: 8, z: 8, core: 2. Of those that a mesh axis runs over, the one named last changes fastest.
Arguments:
- ens_obs: bfloat16 [2048, 256, 2048], P('region', 'member'), may hold values from -6 to 6
- ens_state: bfloat16 [2048, 256, 512], P('region', 'member'), may hold values from -6 to 6
- innovation: float32 [2048, 2048], P('region'), may hold values from -6 to 6
- obs_precision: float32 [2048, 2048], P('region'), may hold values from 0.25 to 4
- obs_count: int32 [2048], P('region'), may hold values from 1 to 1920, as said below
Outputs:
- analysis: bfloat16 [2048, 256, 512], P('region', 'member')
Inputs may be any that keep to these rules, and one draw needn't show every extreme that they name: Tile t uses its first obs_count[t] observation slots. Over every aligned run of 2 tiles, the numbers of 128-slot blocks that hold used slots, ceil(obs_count / 128), sum to at most 16, and to exactly 16 in one run of every aligned four runs.
All inputs are finite; a program needn't handle non-finite values.
Results may differ from a plain program's by a relative error of at most 0.0057.
Values may be sent and summed in bfloat16 or wider, within the bound.
No kernel may reach another device: no remote copies, remote signals or barrier semaphores. Data moves between devices by JAX's collectives and lax.ppermute only.
A program may use at most 32 MiB of HBM per device.

v0:
```python
import jax
import jax.numpy as jnp
from jax import lax
from jax.sharding import PartitionSpec as P

NS_ITERS = 4


def product(left, right):
    return jnp.dot(left, right, precision=lax.Precision.HIGHEST)


def solve_weights(gram_matrix, obs_drive):
    members = gram_matrix.shape[0]
    identity = jnp.eye(members, dtype=jnp.float32)
    system = gram_matrix + (members - 1.0) * identity
    frobenius = jnp.sqrt(jnp.sum(system * system) + 1e-06)
    root_iter = system / frobenius
    inv_root = identity
    for sweep in range(NS_ITERS):
        factor = 1.5 * identity - 0.5 * product(inv_root, root_iter)
        root_iter = product(root_iter, factor)
        inv_root = product(factor, inv_root)
    inverse = product(inv_root, inv_root) / frobenius
    mean_shift = product(inverse, obs_drive)
    root_part = inv_root * jnp.sqrt((members - 1.0) / frobenius)
    return (mean_shift[:, None] + root_part).astype(jnp.bfloat16)


def accumulate(fetch_block, innov, precision, live_count, members):
    block_total = (live_count + 127) // 128

    def add_block(block_index, carry):
        gram_matrix, obs_drive = carry
        first_col = block_index * 128
        block_obs = fetch_block(block_index)
        block_prec = lax.dynamic_slice_in_dim(precision, first_col, 128, 0)
        block_innov = lax.dynamic_slice_in_dim(innov, first_col, 128, 0)
        columns = first_col + jnp.arange(128, dtype=jnp.int32)
        weight = jnp.where(columns < live_count, block_prec, jnp.float32(0.0))
        scaled = (block_obs * weight).astype(jnp.bfloat16)
        gram_matrix = gram_matrix + lax.dot_general(
            scaled, block_obs, (((1,), (1,)), ((), ())), preferred_element_type=jnp.float32
        )
        obs_drive = obs_drive + product(block_obs.astype(jnp.float32), weight * block_innov)
        return (gram_matrix, obs_drive)

    start_carry = (jnp.zeros((members, members), jnp.float32), jnp.zeros((members,), jnp.float32))
    gram_matrix, obs_drive = lax.fori_loop(0, block_total, add_block, start_carry)
    return solve_weights(gram_matrix, obs_drive)


def transform_tile(packed):
    state, weights = packed
    members = state.shape[0]
    average = jnp.sum(state, axis=0, dtype=jnp.float32) / members
    deviation = (state.astype(jnp.float32) - average).astype(jnp.bfloat16)
    moved = lax.dot_general(
        weights, deviation, (((0,), (0,)), ((), ())), preferred_element_type=jnp.float32
    )
    return (average + moved).astype(jnp.bfloat16)


def local(ens_obs, ens_state, innovation, obs_precision, obs_count):
    groups = lax.axis_size("member")
    member_rank = lax.axis_index("member")
    group_tiles = ens_state.shape[0]
    tiles_here = group_tiles // groups
    own_innov = lax.dynamic_slice_in_dim(innovation, member_rank * tiles_here, tiles_here, 0)
    own_prec = lax.dynamic_slice_in_dim(obs_precision, member_rank * tiles_here, tiles_here, 0)
    own_count = lax.dynamic_slice_in_dim(obs_count, member_rank * tiles_here, tiles_here, 0)
    got_obs, got_state = (
        lax.all_to_all(ens_obs, "member", split_axis=0, concat_axis=1, tiled=True),
        lax.all_to_all(ens_state, "member", split_axis=0, concat_axis=1, tiled=True),
    )
    members = got_obs.shape[1]

    def tile_weights(packed):
        observed, innov, precision, live_count = packed

        def fetch_block(block_index):
            return lax.dynamic_slice_in_dim(observed, block_index * 128, 128, 1)

        return accumulate(fetch_block, innov, precision, live_count, members)

    weights = lax.map(tile_weights, (got_obs, own_innov, own_prec, own_count))
    analysed = lax.map(transform_tile, (got_state, weights))
    return lax.all_to_all(analysed, "member", split_axis=1, concat_axis=0, tiled=True)


def solution(mesh):
    placed = (
        P("region", "member", None),
        P("region", "member", None),
        P("region", None),
        P("region", None),
        P("region"),
    )
    return jax.shard_map(
        local, mesh=mesh, in_specs=placed, out_specs=P("region", "member", None), check_vma=False
    )
```

profile of v0, /device:TPU:30, one launch (start us, length us, event | category | flops | bytes accessed | tf_op | source)
XLA Modules:
  0.0 171.9 jit_solution(6835461023733919876)
XLA Ops:
  0.0 35.9 %all_to_all.54 = bf16[64,8,512]{2,1,0:T(8,128)(2,1)S(1)} all-to-all(bf16[64,8,512]{2,1,0:T(8,128)(2,1)} %param.12), channel_id=1, replica_groups=mesh['region'=32,'member'=32] {'member'}, dimensions={0} | all-to-all | bytes 1048576 | tf_op jit(solution)/shard_map/all_to_all | solution.py:74
  35.9 6.5 %all-to-all-start.1 = ((bf16[64,8,2048]{2,1,0:T(8,128)(2,1)}), bf16[64,8,2048]{2,1,0:T(8,128)(2,1)S(1)}, u32[]{:S(2)}, u32[]{:S(2)}) async-start(bf16[64,8,2048]{2,1,0:T(8,128)(2,1)} %param.11), calls=%async_computation.1 | async-start | bytes 4194304 | tf_op jit(solution)/shard_map/all_to_all | solution.py:73
  42.5 0.9 constant_dynamic-slice_fusion.2
  43.4 0.8 copy.16
  44.2 50.0 %all-to-all-done.1 = bf16[64,8,2048]{2,1,0:T(8,128)(2,1)S(1)} async-done(((bf16[64,8,2048]{2,1,0:T(8,128)(2,1)}), bf16[64,8,2048]{2,1,0:T(8,128)(2,1)S(1)}, u32[]{:S(2)}, u32[]{:S(2)}) %all-to-all-start.1) | async-done | bytes 2097184 | tf_op jit(solution)/shard_map/all_to_all | solution.py:73
  94.3 1.3 copy-done
  95.6 1.7 %copy.15 = bf16[32,2,8,2048]{3,2,0,1:T(8,128)(2,1)S(1)} copy(bf16[32,2,8,2048]{3,2,1,0:T(8,128)(2,1)} %bitcast.132) | data formatting | bytes 4194304 | tf_op jit(solution)/shard_map/all_to_all | solution.py:73
  97.4 34.3 %while.47 = (s32[]{:T(128)}, bf16[2,256,256]{2,1,0:T(8,128)(2,1)}, s32[2]{0:T(128)S(1)}, bf16[2,256,2048]{2,1,0:T(8,128)(2,1)S(1)}, f32[2,2048]{1,0:T(2,128)S(1)...) while((s32[]{:T(128)}, bf16[2,256,256]{2,1,0:T(8,128)(2,1)}, ...), condition=%wide.region_4.5_spmd, body=%wide.region_0.4_spmd.sunk | while | flops 2436334336 | bytes 14791922 | solution.py:86
  97.4 0.6 dynamic_slice.94
  98.7 8.7 %while.49 = (s32[]{:T(128)}, f32[256,256]{1,0:T(8,128)S(1)}, f32[256]{0:T(256)S(1)}, s32[]{:T(128)}, bf16[256,2048]{1,0:T(8,128)(2,1)S(1)}, /*index=5*/s32[]{:T(...) while((s32[]{:T(128)}, f32[256,256]{1,0:T(8,128)S(1)}, ...), condition=%wide.region_2.2_spmd, body=%wide.region_1.1_spmd.sunk | while | flops 17335044 | bytes 729775 | solution.py:49
  98.7 0.6 compare_select_fusion.2
  99.8 0.7 compare_select_fusion.2
  100.9 0.7 compare_select_fusion.2
  102.0 0.7 compare_select_fusion.2
  103.0 0.7 compare_select_fusion.2
  104.1 0.7 compare_select_fusion.2
  105.2 0.7 compare_select_fusion.2
  106.3 0.7 compare_select_fusion.2
  107.4 0.7 multiply_reduce_fusion.2
  108.8 0.3 fusion.131
  109.1 0.4 fusion.133
  109.5 0.3 fusion.132
  109.8 0.4 fusion.134
  110.2 0.4 fusion.136
  110.6 0.4 fusion.135
  111.0 0.4 fusion.137
  111.4 0.4 fusion.139
  111.7 0.4 fusion.138
  112.1 0.4 fusion.140
  112.5 0.4 fusion.141
  112.9 0.4 convolution_divide_fusion.2
  113.8 0.7 copy-done.2
  114.5 0.6 dynamic_slice.94
  115.9 8.7 %while.49 = (s32[]{:T(128)}, f32[256,256]{1,0:T(8,128)S(1)}, f32[256]{0:T(256)S(1)}, s32[]{:T(128)}, bf16[256,2048]{1,0:T(8,128)(2,1)S(1)}, /*index=5*/s32[]{:T(...) while((s32[]{:T(128)}, f32[256,256]{1,0:T(8,128)S(1)}, ...), condition=%wide.region_2.2_spmd, body=%wide.region_1.1_spmd.sunk | while | flops 17335044 | bytes 729775 | solution.py:49
  115.9 0.6 compare_select_fusion.2
  116.9 0.7 compare_select_fusion.2
  118.0 0.7 compare_select_fusion.2
  119.1 0.7 compare_select_fusion.2
  120.2 0.7 compare_select_fusion.2
  121.3 0.7 compare_select_fusion.2
  122.4 0.7 compare_select_fusion.2
  123.5 0.7 compare_select_fusion.2
  124.6 0.7 multiply_reduce_fusion.2
  125.9 0.3 fusion.131
  126.3 0.4 fusion.133
  126.7 0.3 fusion.132
  127.0 0.4 fusion.134
  127.3 0.4 fusion.136
  127.7 0.4 fusion.135
  128.1 0.4 fusion.137
  128.5 0.4 fusion.139
  128.9 0.4 fusion.138
  129.3 0.4 fusion.140
  129.7 0.4 fusion.141
  130.1 0.4 convolution_divide_fusion.2
  131.0 0.7 copy-done.2
  131.7 6.0 %while.48 = (s32[]{:T(128)}, bf16[2,256,512]{2,1,0:T(8,128)(2,1)}, bf16[2,256,512]{2,1,0:T(8,128)(2,1)}, bf16[2,256,256]{2,1,0:T(8,128)(2,1)}, s32[]{:T(128)}) while((s32[]{:T(128)}, bf16[2,256,512]{2,1,0:T(8,128)(2,1)}, bf16[2,256,512]{2,1,0:T(8,128)(2,1)}, bf16[2,256,256]{2,1,0:T(8,128)(2,1)}, s32[]{:T(128)}) %tuple.69), condition=%wide.region_7.8_spmd, body=%wide.region_5.7_spmd.sunk | while | flops 68026368 | bytes 929345 | solution.py:87
  131.7 1.0 convert_reduce_fusion.2
  132.7 2.0 %fusion.146 = bf16[2,256,512]{2,1,0:T(8,128)(2,1)} fusion(bf16[2,256,512]{2,1,0:T(8,128)(2,1)} %get-tuple-element.424, s32[]{:T(128)} %get-tuple-element.423, f32[512]{0:T(512)S(1)} %broadcast_multiply_fusion.2, bf16[2,256,512]{2,1,0:T(8,128)(2,1)} %get-tuple-element.430, bf16[2,256,256]{2,1,0:T(8,128)(2,1)} %get-tuple-element.431), kind=kOutput, calls=%fused_computation.40.clone.1 | convolution fusion | flops 67764224 | bytes 660992 | tf_op jit(solution)/shard_map/while/body/eval_jaxpr/dot_general | solution.py:58
  134.7 1.0 convert_reduce_fusion.2
  135.7 2.0 %fusion.146 = bf16[2,256,512]{2,1,0:T(8,128)(2,1)} fusion(bf16[2,256,512]{2,1,0:T(8,128)(2,1)} %get-tuple-element.424, s32[]{:T(128)} %get-tuple-element.423, f32[512]{0:T(512)S(1)} %broadcast_multiply_fusion.2, bf16[2,256,512]{2,1,0:T(8,128)(2,1)} %get-tuple-element.430, bf16[2,256,256]{2,1,0:T(8,128)(2,1)} %get-tuple-element.431), kind=kOutput, calls=%fused_computation.40.clone.1 | convolution fusion | flops 67764224 | bytes 660992 | tf_op jit(solution)/shard_map/while/body/eval_jaxpr/dot_general | solution.py:58
  137.7 1.6 copy.11
  139.3 31.7 %all_to_all.55 = bf16[2,256,512]{2,0,1:T(2,128)(2,1)S(1)} all-to-all(bf16[2,256,512]{2,0,1:T(2,128)(2,1)S(1)} %copy.11), channel_id=1, replica_groups=mesh['region'=32,'member'=32] {'member'}, dimensions={1} | all-to-all | bytes 1048576 | tf_op jit(solution)/shard_map/all_to_all | solution.py:88
  171.0 0.9 copy.12
  (74 shorter events, 7.2 us)
Async XLA Ops:
  35.9 6.5 %copy-start.3 = (s32[64]{0:T(128)S(1)}, s32[64]{0:T(128)}, u32[]{:S(2)}) copy-start(s32[64]{0:T(128)} %param.15) | copy-start | bytes 772
  35.9 58.4 %all-to-all-start.1 = ((bf16[64,8,2048]{2,1,0:T(8,128)(2,1)}), bf16[64,8,2048]{2,1,0:T(8,128)(2,1)S(1)}, u32[]{:S(2)}, u32[]{:S(2)}) async-start(bf16[64,8,2048]{2,1,0:T(8,128)(2,1)} %param.11), calls=%async_computation.1 | async-start | bytes 4194304 | tf_op jit(solution)/shard_map/all_to_all | solution.py:73
  94.3 1.3 copy-start
  111.3 2.4 %copy-start.1 = (bf16[2,256,256]{2,1,0:T(8,128)(2,1)S(1)}, bf16[2,256,256]{2,1,0:T(8,128)(2,1)}, u32[]{:S(2)}) copy-start(bf16[2,256,256]{2,1,0:T(8,128)(2,1)} %get-tuple-element.383) | copy-start | bytes 786436 | tf_op jit(solution)/shard_map/while
  113.8 0.7 copy-start.2
  128.5 2.4 %copy-start.1 = (bf16[2,256,256]{2,1,0:T(8,128)(2,1)S(1)}, bf16[2,256,256]{2,1,0:T(8,128)(2,1)}, u32[]{:S(2)}) copy-start(bf16[2,256,256]{2,1,0:T(8,128)(2,1)} %get-tuple-element.383) | copy-start | bytes 786436 | tf_op jit(solution)/shard_map/while
  131.0 0.7 copy-start.2
where the time goes:
time: 173 us; the launch traced here: 172 us
  blocking collectives  67.7 us (39%)
  waiting for transfers between devices  50 us (29%)
  matrix products  19.2 us (11%)
  other arithmetic  15 us (9%)
  local copies, waits for them, and re-layouts  10.2 us (6%)
  starting transfers between devices  6.48 us (4%)
  loops' own time  3.27 us (2%)
    all_to_all x1, waiting for transfers between devices, local(): lax.all_to_all(ens_obs, 'member', split_axis=0, concat_axis=1, tiled=True)  50 us
    all_to_all x1, blocking collectives, local(): lax.all_to_all(ens_state, 'member', split_axis=0, concat_axis=1, tiled=True)  35.9 us
    all_to_all x1, blocking collectives, local(): lax.all_to_all(analysed, 'member', split_axis=1, concat_axis=0, tiled=True)  31.7 us
    dot_general x42, matrix products, product(): return jnp.dot(left, right, precision=lax.Precision.HIGHEST)  12.1 us
    select_n x16, other arithmetic, add_block(): weight = jnp.where(columns < live_count, block_prec, jnp.float32(0.0))  11.1 us
    all_to_all x1, starting transfers between devices, local(): lax.all_to_all(ens_obs, 'member', split_axis=0, concat_axis=1, tiled=True)  6.48 us
    dot_general x2, matrix products, transform_tile(): lax.dot_general(weights, deviation, (((0,), (0,)), ((), ())), preferred_e...  3.97 us
  transfers between devices with their start and end apart: 1, of which 1 were waited for; matrix products, arithmetic and copies ran while one was open for 1% of the time, Pallas kernels for 0%

commit v1 on v0

v1 whole, which is shorter than its diff:
```python
import jax
import jax.numpy as jnp
from jax import lax
from jax.experimental import pallas as pl
from jax.experimental.pallas import tpu as pltpu
from jax.sharding import PartitionSpec as P

BLOCK = 128
LIVE = 16
SWEEPS = 4
F32, BF16 = jnp.float32, jnp.bfloat16
LAST = (((1,), (1,)), ((), ()))


def pack_kernel(count_ref, obs_ref, state_ref, out_ref, obs_sem, state_sem):
    pairs = out_ref.shape[0]
    state_copy = pltpu.make_async_copy(state_ref, out_ref.at[:, LIVE:], state_sem)
    state_copy.start()

    def start(pair, carry):
        first = lax.shift_right_logical(count_ref[2 * pair] + (BLOCK - 1), 7)
        rest = LIVE - first
        pltpu.make_async_copy(
            obs_ref.at[2 * pair, pl.ds(0, first)], out_ref.at[pair, pl.ds(0, first)], obs_sem
        ).start()
        pltpu.make_async_copy(
            obs_ref.at[2 * pair + 1, pl.ds(0, rest)], out_ref.at[pair, pl.ds(first, rest)], obs_sem
        ).start()
        return carry

    lax.fori_loop(0, pairs, start, 0)
    whole = out_ref.at[:, :LIVE]
    pltpu.make_async_copy(whole, whole, obs_sem).wait()
    state_copy.wait()


def pack(obs_count, ens_obs, ens_state):
    tiles, members, slots = ens_obs.shape
    width = ens_state.shape[2]
    pairs = tiles // 2
    blocks = lambda x, n: x.reshape(tiles, members, n, BLOCK).transpose(0, 2, 1, 3)
    obs = blocks(ens_obs, slots // BLOCK)
    state = blocks(ens_state, width // BLOCK).reshape(pairs, 2 * width // BLOCK, members, BLOCK)
    return pl.pallas_call(
        pack_kernel,
        out_shape=jax.ShapeDtypeStruct((pairs, LIVE + state.shape[1], members, BLOCK), BF16),
        in_specs=[
            pl.BlockSpec(memory_space=pltpu.SMEM),
            pl.BlockSpec(memory_space=pl.ANY),
            pl.BlockSpec(memory_space=pl.ANY),
        ],
        out_specs=pl.BlockSpec(memory_space=pltpu.VMEM),
        scratch_shapes=[pltpu.SemaphoreType.DMA, pltpu.SemaphoreType.DMA],
        name="pack",
    )(obs_count, obs, state)


def split(x):
    high = x.astype(BF16)
    return high, (x - high.astype(F32)).astype(BF16)


def mm(a, b):
    return jnp.dot(a, b, preferred_element_type=F32)


def thirds(x):
    high = x.astype(BF16)
    left = x - high.astype(F32)
    middle = left.astype(BF16)
    low = (left - middle.astype(F32)).astype(BF16)
    return jnp.concatenate([high.astype(F32), middle.astype(F32), low.astype(F32)], axis=0)


def row_times(row, high, low):
    parts = thirds(row)
    lhs = jnp.concatenate([parts, jnp.zeros((5, row.shape[1]), F32)], axis=0).astype(BF16)
    return jnp.sum(mm(lhs, high) + mm(lhs, low), axis=0, keepdims=True)


def analyse_kernel(rank_ref, count_ref, got_ref, innov_ref, prec_ref, out_ref,
                   obs_ref, scaled_ref, line_ref, dev_ref):
    sources, _, each, _ = got_ref.shape
    members = sources * each
    slots = LIVE * BLOCK
    rank = rank_ref[0]
    row = 2 * lax.rem(rank, 4)
    first_blocks = lax.shift_right_logical(count_ref[2 * rank] + (BLOCK - 1), 7)
    column = lax.broadcasted_iota(jnp.int32, (1, slots), 1)

    line_ref[...] = jnp.zeros_like(line_ref)
    for tile in range(2):
        live = column < count_ref[2 * rank + tile]
        weight = jnp.where(live, prec_ref[pl.ds(row + tile, 1), :], 0.0)
        pushed = weight * innov_ref[pl.ds(row + tile, 1), :]
        start = 0 if tile == 0 else pl.multiple_of(first_blocks * BLOCK, BLOCK)
        line_ref[pl.ds(tile, 1), pl.ds(start, slots)] = weight
        line_ref[pl.ds(2 + tile, 1), pl.ds(start, slots)] = pushed

    for block in range(LIVE):
        at = slice(block * BLOCK, (block + 1) * BLOCK)
        values = got_ref[:, block].astype(F32).reshape(members, BLOCK)
        obs_ref[:, at] = values.astype(BF16)
        for tile in range(2):
            scaled_ref[tile, :, at] = (values * line_ref[pl.ds(tile, 1), at]).astype(BF16)

    observed = obs_ref[...]
    lines = jnp.concatenate(
        [thirds(line_ref[pl.ds(2, 1), :slots]), thirds(line_ref[pl.ds(3, 1), :slots]),
         jnp.zeros((2, slots), F32)], axis=0).astype(BF16)
    drives = lax.dot_general(lines, observed, LAST, preferred_element_type=F32)
    drive = [jnp.sum(drives[3 * t:3 * t + 3], axis=0, keepdims=True) for t in range(2)]

    on_diagonal = (lax.broadcasted_iota(jnp.int32, (members, members), 0)
                   == lax.broadcasted_iota(jnp.int32, (members, members), 1))
    eye = jnp.where(on_diagonal, 1.0, 0.0).astype(F32)
    error, root, frob = [], [], []
    for tile in range(2):
        system = lax.dot_general(observed, scaled_ref[tile], LAST, preferred_element_type=F32)
        system = system + (members - 1.0) * eye
        norm = jnp.sqrt(jnp.sum(system * system, keepdims=True) + 1e-06)
        frob.append(norm)
        error.append(system / norm)
        root.append(1.5 * eye - 0.5 * error[tile])

    for sweep in range(1, SWEEPS):
        for tile in range(2):
            e = error[tile]
            e16 = e.astype(BF16)
            g = 1.5 * e - 0.5 * mm(e16, e16)
            e = 1.5 * g - 0.5 * mm(g.astype(BF16), e16)
            error[tile] = e
            z = root[tile]
            root[tile] = 1.5 * z - 0.5 * mm(z.astype(BF16), e.astype(BF16))

    width = out_ref.shape[1] // 2
    for tile in range(2):
        z = root[tile]
        high, low = split(z)
        shift = row_times(row_times(drive[tile], high, low), high, low) / frob[tile]
        transform = (shift + z * jnp.sqrt((members - 1.0) / frob[tile])).astype(BF16)
        averages = []
        for q in range(width):
            state = got_ref[:, LIVE + tile * width + q].astype(F32).reshape(members, BLOCK)
            average = jnp.sum(state, axis=0, keepdims=True) * (1.0 / members)
            averages.append(average)
            dev_ref[:, q * BLOCK:(q + 1) * BLOCK] = (state - average).astype(BF16)
        moved = mm(transform, dev_ref[...])
        for q in range(width):
            result = averages[q] + moved[:, q * BLOCK:(q + 1) * BLOCK]
            out_ref[:, tile * width + q] = result.reshape(sources, each, BLOCK).astype(BF16)


def analyse(rank, obs_count, got, innovation, obs_precision):
    sources, blocks, each, _ = got.shape
    members = sources * each
    slots = innovation.shape[1]
    width = blocks - LIVE
    whole = lambda shape: pl.BlockSpec(shape, lambda i, rank, count: (0,) * len(shape))
    rows = pl.BlockSpec((8, slots), lambda i, rank, count: (lax.div(rank[0], 4), 0))
    return pl.pallas_call(
        analyse_kernel,
        out_shape=jax.ShapeDtypeStruct((sources, width, each, BLOCK), BF16),
        grid_spec=pltpu.PrefetchScalarGridSpec(
            num_scalar_prefetch=2,
            grid=(1,),
            in_specs=[whole(got.shape), rows, rows],
            out_specs=whole((sources, width, each, BLOCK)),
            scratch_shapes=[
                pltpu.VMEM((members, slots), BF16),
                pltpu.VMEM((2, members, slots), BF16),
                pltpu.VMEM((8, 2 * slots), F32),
                pltpu.VMEM((members, width * BLOCK // 2), BF16),
            ],
        ),
        name="analyse",
    )(rank, obs_count, got, innovation, obs_precision)


def local(ens_obs, ens_state, innovation, obs_precision, obs_count):
    tiles, each, variables = ens_state.shape
    rank = lax.axis_index("member").astype(jnp.int32).reshape(1)
    exchange = lambda x: lax.all_to_all(x, "member", split_axis=0, concat_axis=0, tiled=True)
    got = exchange(pack(obs_count, ens_obs, ens_state))
    back = exchange(analyse(rank, obs_count, got, innovation, obs_precision))
    back = back.reshape(tiles, variables // BLOCK, each, BLOCK)
    return back.transpose(0, 2, 1, 3).reshape(tiles, each, variables)


def solution(mesh):
    placed = (
        P("region", "member", None),
        P("region", "member", None),
        P("region", None),
        P("region", None),
        P("region"),
    )
    return jax.shard_map(
        local, mesh=mesh, in_specs=placed, out_specs=P("region", "member", None), check_vma=False
    )
```

time: 173 us -> 95.6 us (0.55)
  the two profiles are of different devices: /device:TPU:30 before, /device:TPU:126 now
where the time goes in v1:
time: 95.6 us; the launch traced here: 95.3 us
  waiting for transfers between devices  38.6 us (40%)
  blocking collectives  24.5 us (26%)
  starting transfers between devices  20.2 us (21%)
  Pallas kernels  10 us (10%)
  local copies, waits for them, and re-layouts  1.97 us (2%)
    all_to_all x1, waiting for transfers between devices, local(): lax.all_to_all(x, 'member', split_axis=0, concat_axis=0, tiled=True)  38.6 us
    all_to_all x1, blocking collectives, local(): lax.all_to_all(x, 'member', split_axis=0, concat_axis=0, tiled=True)  24.5 us
    all_to_all x1, starting transfers between devices, local(): lax.all_to_all(x, 'member', split_axis=0, concat_axis=0, tiled=True)  20.2 us
    pallas_call x1, Pallas kernels, analyse(): pl.pallas_call(analyse_kernel, out_shape=jax.ShapeDtypeStruct((sources, w...  6.77 us
    pallas_call x1, Pallas kernels, pack(): pl.pallas_call(pack_kernel, out_shape=jax.ShapeDtypeStruct((pairs, LIVE +...  3.26 us
    unnamed x3, local copies, waits for them, and re-layouts  1.97 us
  transfers between devices with their start and end apart: 1, of which 1 were waited for; matrix products, arithmetic and copies ran while one was open for 0% of the time, Pallas kernels for 0%

profile of v1, /device:TPU:126, one launch (start us, length us, event | category | flops | bytes accessed | tf_op | source)
XLA Modules:
  0.0 95.3 jit_solution(18168692321834795060)
XLA Ops:
  0.0 3.3 %pack.1 = bf16[32,24,8,128]{3,2,1,0:T(8,128)(2,1)} custom-call(s32[64]{0:T(128)} %count_ref.3, bf16[64,16,8,128]{3,2,1,0:T(8,128)(2,1)} %bitcast.14, bf16[32,8,8,128]{3,2,1,0:T(8,128)(2,1)} %bitcast.16), custom_call_target="tpu_custom_call" | custom-call | tf_op jit(solution)/shard_map/pack/pallas_call | solution.py:44
  3.3 20.2 %all-to-all-start = ((bf16[32,24,8,128]{3,2,1,0:T(8,128)(2,1)}), bf16[32,24,8,128]{3,2,1,0:T(8,128)(2,1)S(1)}, u32[]{:S(2)}, u32[]{:S(2)}) async-start(bf16[32,24,8,128]{3,2,1,0:T(8,128)(2,1)} %pack.1), calls=%async_computation | async-start | bytes 3145728 | tf_op jit(solution)/shard_map/all_to_all | solution.py:183
  23.4 38.6 %all-to-all-done.got_ref = bf16[32,24,8,128]{3,2,1,0:T(8,128)(2,1)S(1)} async-done(((bf16[32,24,8,128]{3,2,1,0:T(8,128)(2,1)}), bf16[32,24,8,128]{3,2,1,0:T(8,128)(2,1)S(1)}, u32[]{:S(2)}, u32[]{:S(2)}) %all-to-all-start) | async-done | bytes 1572896 | tf_op jit(solution)/shard_map/all_to_all | solution.py:183
  62.0 0.0 copy-start
  62.0 1.2 %copy-done = bf16[32,24,8,128]{3,2,1,0:T(8,128)(2,1)} copy-done((bf16[32,24,8,128]{3,2,1,0:T(8,128)(2,1)}, bf16[32,24,8,128]{3,2,1,0:T(8,128)(2,1)S(1)}, u32[]{:S(2)}) %copy-start) | copy-done | bytes 1572888
  63.2 6.8 %analyse.1 = bf16[32,8,8,128]{3,2,1,0:T(8,128)(2,1)} custom-call(s32[1]{0:T(128)} %bitcast.rank_ref, s32[64]{0:T(128)} %count_ref.3, bf16[32,24,8,128]{3,2,1,0:T(8,128)(2,1)} %copy-done, f32[64,2048]{1,0:T(8,128)} %innov_ref.1, f32[64,2048]{1,0:T(8,128)} %prec_ref.1), custom_call_target="tpu_custom_call" | custom-call | tf_op jit(solution)/shard_map/analyse/pallas_call | solution.py:161
  69.9 24.5 %all_to_all.10 = bf16[32,8,8,128]{3,2,1,0:T(8,128)(2,1)S(1)} all-to-all(bf16[32,8,8,128]{3,2,1,0:T(8,128)(2,1)} %analyse.1), channel_id=1, replica_groups=mesh['region'=32,'member'=32] {'member'}, dimensions={0} | all-to-all | bytes 1048576 | tf_op jit(solution)/shard_map/all_to_all | solution.py:183
  94.5 0.8 copy.7
Async XLA Ops:
  3.3 58.7 %all-to-all-start = ((bf16[32,24,8,128]{3,2,1,0:T(8,128)(2,1)}), bf16[32,24,8,128]{3,2,1,0:T(8,128)(2,1)S(1)}, u32[]{:S(2)}, u32[]{:S(2)}) async-start(bf16[32,24,8,128]{3,2,1,0:T(8,128)(2,1)} %pack.1), calls=%async_computation | async-start | bytes 3145728 | tf_op jit(solution)/shard_map/all_to_all | solution.py:183
  62.0 1.2 %copy-start = (bf16[32,24,8,128]{3,2,1,0:T(8,128)(2,1)}, bf16[32,24,8,128]{3,2,1,0:T(8,128)(2,1)S(1)}, u32[]{:S(2)}) copy-start(bf16[32,24,8,128]{3,2,1,0:T(8,128)(2,1)S(1)} %all-to-all-done.got_ref) | copy-start | bytes 4718596

commit v2 on v1

v2 whole, which is shorter than its diff:
```python
import jax
import jax.numpy as jnp
from jax import lax
from jax.experimental import pallas as pl
from jax.experimental.pallas import tpu as pltpu
from jax.sharding import PartitionSpec as P

BLOCK = 128
LIVE = 16
F32, BF16 = jnp.float32, jnp.bfloat16
LAST = (((1,), (1,)), ((), ()))


def pack_kernel(count_ref, obs_ref, state_ref, out_ref, obs_sem, state_sem):
    pairs = out_ref.shape[0]
    state_copy = pltpu.make_async_copy(state_ref, out_ref.at[:, LIVE:], state_sem)
    state_copy.start()

    def start(pair, carry):
        first = lax.shift_right_logical(count_ref[2 * pair] + (BLOCK - 1), 7)
        rest = LIVE - first
        pltpu.make_async_copy(
            obs_ref.at[2 * pair, pl.ds(0, first)], out_ref.at[pair, pl.ds(0, first)], obs_sem
        ).start()
        pltpu.make_async_copy(
            obs_ref.at[2 * pair + 1, pl.ds(0, rest)], out_ref.at[pair, pl.ds(first, rest)], obs_sem
        ).start()
        return carry

    lax.fori_loop(0, pairs, start, 0)
    whole = out_ref.at[:, :LIVE]
    pltpu.make_async_copy(whole, whole, obs_sem).wait()
    state_copy.wait()


def pack(obs_count, ens_obs, ens_state):
    tiles, members, slots = ens_obs.shape
    width = ens_state.shape[2]
    pairs = tiles // 2
    blocks = lambda x, n: x.reshape(tiles, members, n, BLOCK).transpose(0, 2, 1, 3)
    obs = blocks(ens_obs, slots // BLOCK)
    state = blocks(ens_state, width // BLOCK).reshape(pairs, 2 * width // BLOCK, members, BLOCK)
    return pl.pallas_call(
        pack_kernel,
        out_shape=pltpu.VMEM((pairs, LIVE + state.shape[1], members, BLOCK), BF16),
        in_specs=[
            pl.BlockSpec(memory_space=pltpu.SMEM),
            pl.BlockSpec(memory_space=pl.ANY),
            pl.BlockSpec(memory_space=pl.ANY),
        ],
        out_specs=pl.BlockSpec(memory_space=pltpu.VMEM),
        scratch_shapes=[pltpu.SemaphoreType.DMA, pltpu.SemaphoreType.DMA],
        name="pack",
    )(obs_count, obs, state)


def mm(a, b):
    return jnp.dot(a.astype(BF16), b.astype(BF16), preferred_element_type=F32)


def thirds(x):
    high = x.astype(BF16).astype(F32)
    middle = (x - high).astype(BF16).astype(F32)
    return [high, middle, x - high - middle]


C0, C1, C2, C3, C4 = 2.25, -2.4375, 1.6875, -0.5625, 0.0625


def analyse_kernel(rank_ref, count_ref, got_ref, innov_ref, prec_ref, out_ref, line_ref):
    sources, blocks, each, _ = got_ref.shape
    members = sources * each
    slots = LIVE * BLOCK
    width = (blocks - LIVE) // 2
    rank = rank_ref[0]
    row = 2 * lax.rem(rank, 4)
    first_slots = pl.multiple_of(
        lax.shift_right_logical(count_ref[2 * rank] + (BLOCK - 1), 7) * BLOCK, BLOCK)
    column = lax.broadcasted_iota(jnp.int32, (1, slots), 1)

    line_ref[...] = jnp.zeros_like(line_ref)
    for tile in range(2):
        live = column < count_ref[2 * rank + tile]
        weight = jnp.where(live, prec_ref[pl.ds(row + tile, 1), :], 0.0)
        pushed = weight * innov_ref[pl.ds(row + tile, 1), :]
        start = 0 if tile == 0 else first_slots
        line_ref[pl.ds(tile, 1), pl.ds(start, slots)] = weight
        line_ref[pl.ds(2 + tile, 1), pl.ds(start, slots)] = pushed

    weights = [line_ref[pl.ds(t, 1), :slots] for t in range(2)]
    parts = thirds(line_ref[pl.ds(2, 1), :slots]) + thirds(line_ref[pl.ds(3, 1), :slots])
    pushes = jnp.concatenate(parts + [jnp.zeros((10, slots), F32)], axis=0).astype(BF16)

    observed, scaled = [], [[], []]
    for block in range(LIVE):
        at = slice(block * BLOCK, (block + 1) * BLOCK)
        values = got_ref[:, block].reshape(members, BLOCK)
        observed.append(values)
        for tile in range(2):
            scaled[tile].append((values.astype(F32) * weights[tile][:, at]).astype(BF16))
    observed = jnp.concatenate(observed, axis=1)
    left = jnp.concatenate(
        [jnp.concatenate(scaled[0], axis=1), jnp.concatenate(scaled[1], axis=1), pushes], axis=0)
    sums = lax.dot_general(left, observed, LAST, preferred_element_type=F32)
    drives = sums[2 * members:]
    drive = [jnp.sum(drives[3 * t:3 * t + 3], axis=0, keepdims=True) for t in range(2)]

    on_diagonal = (lax.broadcasted_iota(jnp.int32, (members, members), 0)
                   == lax.broadcasted_iota(jnp.int32, (members, members), 1))
    unit, frob = [], []
    for t in range(2):
        system = sums[t * members:(t + 1) * members]
        system = jnp.where(on_diagonal, system + (members - 1.0), system)
        norm = jnp.sqrt(jnp.sum(system * system, keepdims=True) + 1e-06)
        frob.append(norm)
        unit.append(system / norm)

    def sweeps(e):
        square = [mm(x, x) for x in e]
        tail = [mm(q, C3 * x + C4 * q) for q, x in zip(square, e)]
        return [C1 * x + C2 * q + r for x, q, r in zip(e, square, tail)]

    first = sweeps(unit)
    moved_y = [C0 * x + mm(x, d) for x, d in zip(unit, first)]
    second = sweeps([C0 * y + mm(y, d) for y, d in zip(moved_y, first)])
    rest = [C0 * (d + q) + mm(d, q) for d, q in zip(first, second)]

    averages, deviations = [[], []], [[], []]
    for t in range(2):
        for q in range(width):
            state = got_ref[:, LIVE + t * width + q].reshape(members, BLOCK).astype(F32)
            average = jnp.sum(state, axis=0, keepdims=True) * (1.0 / members)
            averages[t].append(average)
            deviations[t].append((state - average).astype(BF16))

    for t in range(2):
        root = jnp.where(on_diagonal, rest[t] + C0 * C0, rest[t])
        once = jnp.sum(root * drive[t], axis=1, keepdims=True)
        shift = jnp.sum(root * once, axis=0, keepdims=True) / frob[t]
        scale = jnp.sqrt((members - 1.0) / frob[t])
        transform = (shift + root * scale).astype(BF16)
        moved = mm(transform, jnp.concatenate(deviations[t], axis=1))
        for q in range(width):
            result = averages[t][q] + moved[:, q * BLOCK:(q + 1) * BLOCK]
            out_ref[:, t * width + q] = result.astype(BF16).reshape(sources, each, BLOCK)


def analyse(rank, obs_count, got, innovation, obs_precision):
    sources, blocks, each, _ = got.shape
    slots = innovation.shape[1]
    rows = pl.BlockSpec((8, slots), lambda i, rank, count: (lax.div(rank[0], 4), 0))
    vmem = pl.BlockSpec(memory_space=pltpu.VMEM)
    return pl.pallas_call(
        analyse_kernel,
        out_shape=pltpu.VMEM((sources, blocks - LIVE, each, BLOCK), BF16),
        grid_spec=pltpu.PrefetchScalarGridSpec(
            num_scalar_prefetch=2,
            grid=(1,),
            in_specs=[vmem, rows, rows],
            out_specs=vmem,
            scratch_shapes=[pltpu.VMEM((8, 2 * slots), F32)],
        ),
        name="analyse",
    )(rank, obs_count, pltpu.with_memory_space_constraint(got, pltpu.VMEM), innovation, obs_precision)


def local(ens_obs, ens_state, innovation, obs_precision, obs_count):
    tiles, each, variables = ens_state.shape
    rank = lax.axis_index("member").astype(jnp.int32).reshape(1)
    exchange = lambda x: lax.all_to_all(x, "member", split_axis=0, concat_axis=0, tiled=True)
    packed, rank = lax.optimization_barrier((pack(obs_count, ens_obs, ens_state), rank))
    got = exchange(packed)
    back = exchange(analyse(rank, obs_count, got, innovation, obs_precision))
    back = back.reshape(tiles, variables // BLOCK, each, BLOCK)
    return back.transpose(0, 2, 1, 3).reshape(tiles, each, variables)


def solution(mesh):
    placed = (
        P("region", "member", None),
        P("region", "member", None),
        P("region", None),
        P("region", None),
        P("region"),
    )
    return jax.shard_map(
        local, mesh=mesh, in_specs=placed, out_specs=P("region", "member", None), check_vma=False
    )
```

time: 95.6 us -> 88.9 us (0.930)
  the two profiles are of different devices: /device:TPU:126 before, /device:TPU:66 now
where the time goes in v2:
time: 88.9 us; the launch traced here: 88.6 us
  blocking collectives  80.9 us (91%)
  Pallas kernels  6.9 us (8%)
    all_to_all x2, blocking collectives, local(): lax.all_to_all(x, 'member', split_axis=0, concat_axis=0, tiled=True)  80.9 us
    pallas_call x1, Pallas kernels, analyse(): pl.pallas_call(analyse_kernel, out_shape=pltpu.VMEM((sources, blocks - LI...  4.81 us
    pallas_call x1, Pallas kernels, pack(): pl.pallas_call(pack_kernel, out_shape=pltpu.VMEM((pairs, LIVE + state.sha...  2.08 us

profile of v2, /device:TPU:66, one launch (start us, length us, event | category | flops | bytes accessed | tf_op | source)
XLA Modules:
  0.0 88.6 jit_solution(6269883940707727748)
XLA Ops:
  0.0 2.1 %pack.1 = bf16[32,24,8,128]{3,2,1,0:T(8,128)(2,1)S(1)} custom-call(s32[64]{0:T(128)} %count_ref.3, bf16[64,16,8,128]{3,2,1,0:T(8,128)(2,1)} %bitcast.14, bf16[32,8,8,128]{3,2,1,0:T(8,128)(2,1)} %bitcast.16), custom_call_target="tpu_custom_call" | custom-call | tf_op jit(solution)/shard_map/pack/pallas_call | solution.py:43
  2.1 59.1 %all_to_all.10.got_ref = bf16[32,24,8,128]{3,2,1,0:T(8,128)(2,1)S(1)} all-to-all(bf16[32,24,8,128]{3,2,1,0:T(8,128)(2,1)S(1)} %pack.1), channel_id=1, replica_groups=mesh['region'=32,'member'=32] {'member'}, dimensions={0} | all-to-all | bytes 3145728 | tf_op jit(solution)/shard_map/all_to_all | solution.py:170
  61.2 4.8 %analyse.1 = bf16[32,8,8,128]{3,2,1,0:T(8,128)(2,1)S(1)} custom-call(s32[1]{0:T(128)} %bitcast.5.rank_ref, s32[64]{0:T(128)} %count_ref.3, bf16[32,24,8,128]{3,2,1,0:T(8,128)(2,1)S(1)} %all_to_all.10.got_ref, f32[64,2048]{1,0:T(8,128)} %innov_ref.1, f32[64,2048]{1,0:T(8,128)} %prec_ref.1), custom_call_target="tpu_custom_call" | custom-call | tf_op jit(solution)/shard_map/analyse/pallas_call | solution.py:153
  66.0 21.9 %all_to_all.11 = bf16[32,8,8,128]{3,2,1,0:T(8,128)(2,1)S(1)} all-to-all(bf16[32,8,8,128]{3,2,1,0:T(8,128)(2,1)S(1)} %analyse.1), channel_id=1, replica_groups=mesh['region'=32,'member'=32] {'member'}, dimensions={0} | all-to-all | bytes 1048576 | tf_op jit(solution)/shard_map/all_to_all | solution.py:170
  87.8 0.8 copy.7

commit v3 on v2

v3 whole, which is shorter than its diff:
```python
import jax
import jax.numpy as jnp
from jax import lax
from jax.experimental import pallas as pl
from jax.experimental.pallas import tpu as pltpu
from jax.sharding import PartitionSpec as P

BLOCK = 128
LIVE = 16
STEP = 4
F32, BF16 = jnp.float32, jnp.bfloat16
LAST = (((1,), (1,)), ((), ()))


def thirds(x):
    high = x.astype(BF16).astype(F32)
    middle = (x - high).astype(BF16).astype(F32)
    return [high, middle, x - high - middle]


def blocks_used(count):
    return lax.shift_right_logical(count + (BLOCK - 1), 7)


def pack_kernel(rank_ref, count_ref, obs_ref, state_ref, innov_ref, prec_ref,
                out_ref, weight_ref, push_ref,
                innov_rows, prec_rows, line_ref, obs_sem, state_sem, innov_sem, prec_sem):
    pairs = out_ref.shape[0]
    slots = LIVE * BLOCK
    rank = rank_ref[0]
    eight = pl.ds(pl.multiple_of(8 * lax.div(rank, 4), 8), 8)
    copies = [
        pltpu.make_async_copy(state_ref, out_ref.at[:, LIVE:], state_sem),
        pltpu.make_async_copy(innov_ref.at[eight], innov_rows, innov_sem),
        pltpu.make_async_copy(prec_ref.at[eight], prec_rows, prec_sem),
    ]
    for copy in copies:
        copy.start()

    def start(pair, carry):
        first = blocks_used(count_ref[2 * pair])
        rest = LIVE - first
        pltpu.make_async_copy(
            obs_ref.at[2 * pair, pl.ds(0, first)], out_ref.at[pair, pl.ds(0, first)], obs_sem
        ).start()
        pltpu.make_async_copy(
            obs_ref.at[2 * pair + 1, pl.ds(0, rest)], out_ref.at[pair, pl.ds(first, rest)], obs_sem
        ).start()
        return carry

    lax.fori_loop(0, pairs, start, 0)

    row = 2 * lax.rem(rank, 4)
    first = blocks_used(count_ref[2 * rank])
    column = lax.broadcasted_iota(jnp.int32, (1, slots), 1)
    line_ref[...] = jnp.zeros_like(line_ref)
    for copy in copies[1:]:
        copy.wait()
    for tile in range(2):
        live = column < count_ref[2 * rank + tile]
        weight = jnp.where(live, prec_rows[pl.ds(row + tile, 1), :], 0.0)
        begin = 0 if tile == 0 else pl.multiple_of(first * BLOCK, BLOCK)
        line_ref[pl.ds(tile, 1), pl.ds(begin, slots)] = weight
        line_ref[pl.ds(2 + tile, 1), pl.ds(begin, slots)] = weight * innov_rows[pl.ds(row + tile, 1), :]
    weight_ref[:2] = line_ref[:2, :slots]
    weight_ref[2:] = jnp.full((6, slots), first.astype(F32))
    parts = thirds(line_ref[pl.ds(2, 1), :slots]) + thirds(line_ref[pl.ds(3, 1), :slots])
    push_ref[...] = jnp.concatenate(parts + [jnp.zeros((10, slots), F32)], axis=0).astype(BF16)

    whole = out_ref.at[:, :LIVE]
    pltpu.make_async_copy(whole, whole, obs_sem).wait()
    copies[0].wait()


def pack(rank, obs_count, ens_obs, ens_state, innovation, obs_precision):
    tiles, members, slots = ens_obs.shape
    width = ens_state.shape[2]
    pairs = tiles // 2
    blocks = lambda x, n: x.reshape(tiles, members, n, BLOCK).transpose(0, 2, 1, 3)
    obs = blocks(ens_obs, slots // BLOCK)
    state = blocks(ens_state, width // BLOCK).reshape(pairs, 2 * width // BLOCK, members, BLOCK)
    smem, hbm, vmem = (pl.BlockSpec(memory_space=m) for m in (pltpu.SMEM, pl.ANY, pltpu.VMEM))
    return pl.pallas_call(
        pack_kernel,
        out_shape=(
            pltpu.VMEM((pairs, LIVE + state.shape[1], members, BLOCK), BF16),
            pltpu.VMEM((8, slots), F32),
            pltpu.VMEM((16, slots), BF16),
        ),
        in_specs=[smem, smem, hbm, hbm, hbm, hbm],
        out_specs=(vmem, vmem, vmem),
        scratch_shapes=[
            pltpu.VMEM((8, slots), F32),
            pltpu.VMEM((8, slots), F32),
            pltpu.VMEM((8, 2 * slots), F32),
        ] + [pltpu.SemaphoreType.DMA] * 4,
        name="pack",
    )(rank, obs_count, obs, state, innovation, obs_precision)


def mm(a, b):
    return jnp.dot(a.astype(BF16), b.astype(BF16), preferred_element_type=F32)


C0, C1, C2, C3, C4 = 2.25, -2.4375, 1.6875, -0.5625, 0.0625


def analyse_kernel(got_ref, weight_ref, push_ref, out_ref, sum_ref):
    sources, blocks, each, _ = got_ref.shape
    members = sources * each
    width = (blocks - LIVE) // 2

    def values_of(block):
        return got_ref[:, block].reshape(members, BLOCK)

    def product(first, last, tiles):
        observed = [values_of(block) for block in range(first, last)]
        at = slice(first * BLOCK, last * BLOCK)
        rows = []
        for tile in tiles:
            rows.append(jnp.concatenate(
                [(x.astype(F32) * weight_ref[pl.ds(tile, 1), pl.ds((first + i) * BLOCK, BLOCK)]).astype(BF16)
                 for i, x in enumerate(observed)], axis=1))
        left = jnp.concatenate(rows + [push_ref[:, at]], axis=0)
        return lax.dot_general(
            left, jnp.concatenate(observed, axis=1), LAST, preferred_element_type=F32)

    stretch = lax.div(jnp.max(weight_ref[pl.ds(2, 1), :BLOCK]).astype(jnp.int32), STEP)
    for part in range(LIVE // STEP):
        low, high = part * STEP, (part + 1) * STEP

        @pl.when(stretch == part)
        def _():
            middle = product(low, high, (0, 1))
            first, second, lines = middle[:members], middle[members:2 * members], middle[2 * members:]
            if low:
                more = product(0, low, (0,))
                first, lines = first + more[:members], lines + more[members:]
            if high < LIVE:
                more = product(high, LIVE, (1,))
                second, lines = second + more[:members], lines + more[members:]
            sum_ref[:members] = first
            sum_ref[members:2 * members] = second
            sum_ref[2 * members:] = lines

    drives = sum_ref[2 * members:]
    drive = [jnp.sum(drives[3 * t:3 * t + 3], axis=0, keepdims=True) for t in range(2)]

    averages, deviations = [[], []], [[], []]
    waiting = [(t, q) for t in range(2) for q in range(width)]

    def prepare(count):
        for t, q in waiting[:count]:
            state = values_of(LIVE + t * width + q).astype(F32)
            average = jnp.sum(state, axis=0, keepdims=True) * (1.0 / members)
            averages[t].append(average)
            deviations[t].append((state - average).astype(BF16))
        del waiting[:count]

    on_diagonal = (lax.broadcasted_iota(jnp.int32, (members, members), 0)
                   == lax.broadcasted_iota(jnp.int32, (members, members), 1))
    unit, square, frob = [], [], []
    for t in range(2):
        system = sum_ref[t * members:(t + 1) * members]
        system = jnp.where(on_diagonal, system + (members - 1.0), system)
        raw = mm(system, system)
        norm = jnp.sqrt(jnp.sum(system * system, keepdims=True) + 1e-06)
        inverse = 1.0 / norm
        frob.append(norm)
        unit.append(system * inverse)
        square.append(raw * (inverse * inverse))
    prepare(2)

    def sweeps(e, square):
        tail = [mm(q, C3 * x + C4 * q) for q, x in zip(square, e)]
        return [C1 * x + C2 * q + r for x, q, r in zip(e, square, tail)]

    first = sweeps(unit, square)
    prepare(2)
    moved_y = [C0 * x + mm(x, d) for x, d in zip(unit, first)]
    prepare(2)
    error = [C0 * y + mm(y, d) for y, d in zip(moved_y, first)]
    prepare(2)
    second = sweeps(error, [mm(x, x) for x in error])
    rest = [C0 * (d + q) + mm(d, q) for d, q in zip(first, second)]

    for t in range(2):
        root = jnp.where(on_diagonal, rest[t] + C0 * C0, rest[t])
        once = jnp.sum(root * drive[t], axis=1, keepdims=True)
        shift = jnp.sum(root * once, axis=0, keepdims=True) / frob[t]
        scale = jnp.sqrt((members - 1.0) / frob[t])
        transform = (shift + root * scale).astype(BF16)
        moved = mm(transform, jnp.concatenate(deviations[t], axis=1))
        for q in range(width):
            result = averages[t][q] + moved[:, q * BLOCK:(q + 1) * BLOCK]
            out_ref[:, t * width + q] = result.astype(BF16).reshape(sources, each, BLOCK)


def analyse(got, weights, pushes):
    sources, blocks, each, _ = got.shape
    members = sources * each
    vmem = pl.BlockSpec(memory_space=pltpu.VMEM)
    here = lambda x: pltpu.with_memory_space_constraint(x, pltpu.VMEM)
    return pl.pallas_call(
        analyse_kernel,
        out_shape=pltpu.VMEM((sources, blocks - LIVE, each, BLOCK), BF16),
        in_specs=[vmem, vmem, vmem],
        out_specs=vmem,
        scratch_shapes=[pltpu.VMEM((2 * members + 16, members), F32)],
        name="analyse",
    )(here(got), here(weights), here(pushes))


def local(ens_obs, ens_state, innovation, obs_precision, obs_count):
    tiles, each, variables = ens_state.shape
    rank = lax.axis_index("member").astype(jnp.int32).reshape(1)
    exchange = lambda x: lax.all_to_all(x, "member", split_axis=0, concat_axis=0, tiled=True)
    packed, weights, pushes = pack(
        rank, obs_count, ens_obs, ens_state, innovation, obs_precision)
    back = exchange(analyse(exchange(packed), weights, pushes))
    back = back.reshape(tiles, variables // BLOCK, each, BLOCK)
    return back.transpose(0, 2, 1, 3).reshape(tiles, each, variables)


def solution(mesh):
    placed = (
        P("region", "member", None),
        P("region", "member", None),
        P("region", None),
        P("region", None),
        P("region"),
    )
    return jax.shard_map(
        local, mesh=mesh, in_specs=placed, out_specs=P("region", "member", None), check_vma=False
    )
```

time: 88.9 us -> 86.8 us (0.976)
  the two profiles are of different devices: /device:TPU:66 before, /device:TPU:82 now
where the time goes in v3:
time: 86.8 us; the launch traced here: 86.6 us
  blocking collectives  80.9 us (93%)
  Pallas kernels  4.82 us (6%)
    all_to_all x2, blocking collectives, local(): lax.all_to_all(x, 'member', split_axis=0, concat_axis=0, tiled=True)  80.9 us
    pallas_call x1, Pallas kernels, analyse(): pl.pallas_call(analyse_kernel, out_shape=pltpu.VMEM((sources, blocks - LI...  2.69 us
    pallas_call x1, Pallas kernels, pack(): pl.pallas_call(pack_kernel, out_shape=(pltpu.VMEM((pairs, LIVE + state.sh...  2.13 us

profile of v3, /device:TPU:82, one launch (start us, length us, event | category | flops | bytes accessed | tf_op | source)
XLA Modules:
  0.0 86.6 jit_solution(16184217643686690286)
XLA Ops:
  0.0 2.1 %pack.1 = (bf16[32,24,8,128]{3,2,1,0:T(8,128)(2,1)S(1)}, f32[8,2048]{1,0:T(8,128)S(1)}, bf16[16,2048]{1,0:T(8,128)(2,1)S(1)}) custom-call(s32[1]{0:T(128)} %bitcast.rank_ref, s32[64]{0:T(128)} %count_ref.1, bf16[64,16,8,128]{3,2,1,0:T(8,128)(2,1)} %bitcast.14, bf16[32,8,8,128]{3,2,1,0:T(8,128)(2,1)} %bitcast.16, f32[64,2048]{1,0:T(8,128)} %innov_ref.1, ...), custom_call_target="tpu_custom_call" | custom-call | tf_op jit(solution)/shard_map/pack/pallas_call | solution.py:83
  2.1 59.1 %all_to_all.10.got_ref = bf16[32,24,8,128]{3,2,1,0:T(8,128)(2,1)S(1)} all-to-all(bf16[32,24,8,128]{3,2,1,0:T(8,128)(2,1)S(1)} %get-tuple-element.8), channel_id=1, replica_groups=mesh['region'=32,'member'=32] {'member'}, dimensions={0} | all-to-all | bytes 3145728 | tf_op jit(solution)/shard_map/all_to_all | solution.py:217
  61.2 2.7 %analyse.1 = bf16[32,8,8,128]{3,2,1,0:T(8,128)(2,1)S(1)} custom-call(bf16[32,24,8,128]{3,2,1,0:T(8,128)(2,1)S(1)} %all_to_all.10.got_ref, f32[8,2048]{1,0:T(8,128)S(1)} %get-tuple-element.9.weight_ref, bf16[16,2048]{1,0:T(8,128)(2,1)S(1)} %get-tuple-element.10.push_ref), custom_call_target="tpu_custom_call" | custom-call | tf_op jit(solution)/shard_map/analyse/pallas_call | solution.py:204
  63.9 21.9 %all_to_all.11 = bf16[32,8,8,128]{3,2,1,0:T(8,128)(2,1)S(1)} all-to-all(bf16[32,8,8,128]{3,2,1,0:T(8,128)(2,1)S(1)} %analyse.1), channel_id=1, replica_groups=mesh['region'=32,'member'=32] {'member'}, dimensions={0} | all-to-all | bytes 1048576 | tf_op jit(solution)/shard_map/all_to_all | solution.py:217
  85.8 0.8 copy.7

commit v4 on v3

--- a/solution.py
+++ b/solution.py
@@ -172,17 +172,17 @@
     prepare(2)
 
     def sweeps(e, square):
-        tail = [mm(q, C3 * x + C4 * q) for q, x in zip(square, e)]
+        tail = [mm(C3 * x + C4 * q, q) for q, x in zip(square, e)]
         return [C1 * x + C2 * q + r for x, q, r in zip(e, square, tail)]
 
     first = sweeps(unit, square)
     prepare(2)
-    moved_y = [C0 * x + mm(x, d) for x, d in zip(unit, first)]
+    moved_y = [C0 * x + mm(d, x) for x, d in zip(unit, first)]
     prepare(2)
     error = [C0 * y + mm(y, d) for y, d in zip(moved_y, first)]
     prepare(2)
     second = sweeps(error, [mm(x, x) for x in error])
-    rest = [C0 * (d + q) + mm(d, q) for d, q in zip(first, second)]
+    rest = [C0 * (d + q) + mm(q, d) for d, q in zip(first, second)]
 
     for t in range(2):
         root = jnp.where(on_diagonal, rest[t] + C0 * C0, rest[t])

time: 86.8 us -> 86.5 us (level)
  the two profiles are of different devices: /device:TPU:82 before, /device:TPU:18 now
where the time goes in v4:
time: 86.5 us; the launch traced here: 86.2 us
  blocking collectives  80.8 us (93%)
  Pallas kernels  4.57 us (5%)
    all_to_all x2, blocking collectives, local(): lax.all_to_all(x, 'member', split_axis=0, concat_axis=0, tiled=True)  80.8 us
    pallas_call x1, Pallas kernels, analyse(): pl.pallas_call(analyse_kernel, out_shape=pltpu.VMEM((sources, blocks - LI...  2.45 us
    pallas_call x1, Pallas kernels, pack(): pl.pallas_call(pack_kernel, out_shape=(pltpu.VMEM((pairs, LIVE + state.sh...  2.12 us

profile of v4, /device:TPU:18, one launch (start us, length us, event | category | flops | bytes accessed | tf_op | source)
XLA Modules:
  0.0 86.2 jit_solution(13358036522718034367)
XLA Ops:
  0.0 2.1 %pack.1 = (bf16[32,24,8,128]{3,2,1,0:T(8,128)(2,1)S(1)}, f32[8,2048]{1,0:T(8,128)S(1)}, bf16[16,2048]{1,0:T(8,128)(2,1)S(1)}) custom-call(s32[1]{0:T(128)} %bitcast.rank_ref, s32[64]{0:T(128)} %count_ref.1, bf16[64,16,8,128]{3,2,1,0:T(8,128)(2,1)} %bitcast.14, bf16[32,8,8,128]{3,2,1,0:T(8,128)(2,1)} %bitcast.16, f32[64,2048]{1,0:T(8,128)} %innov_ref.1, ...), custom_call_target="tpu_custom_call" | custom-call | tf_op jit(solution)/shard_map/pack/pallas_call | solution.py:83
  2.1 59.1 %all_to_all.10.got_ref = bf16[32,24,8,128]{3,2,1,0:T(8,128)(2,1)S(1)} all-to-all(bf16[32,24,8,128]{3,2,1,0:T(8,128)(2,1)S(1)} %get-tuple-element.8), channel_id=1, replica_groups=mesh['region'=32,'member'=32] {'member'}, dimensions={0} | all-to-all | bytes 3145728 | tf_op jit(solution)/shard_map/all_to_all | solution.py:217
  61.2 2.4 %analyse.1 = bf16[32,8,8,128]{3,2,1,0:T(8,128)(2,1)S(1)} custom-call(bf16[32,24,8,128]{3,2,1,0:T(8,128)(2,1)S(1)} %all_to_all.10.got_ref, f32[8,2048]{1,0:T(8,128)S(1)} %get-tuple-element.9.weight_ref, bf16[16,2048]{1,0:T(8,128)(2,1)S(1)} %get-tuple-element.10.push_ref), custom_call_target="tpu_custom_call" | custom-call | tf_op jit(solution)/shard_map/analyse/pallas_call | solution.py:204
  63.7 21.7 %all_to_all.11 = bf16[32,8,8,128]{3,2,1,0:T(8,128)(2,1)S(1)} all-to-all(bf16[32,8,8,128]{3,2,1,0:T(8,128)(2,1)S(1)} %analyse.1), channel_id=1, replica_groups=mesh['region'=32,'member'=32] {'member'}, dimensions={0} | all-to-all | bytes 1048576 | tf_op jit(solution)/shard_map/all_to_all | solution.py:217
  85.4 0.8 copy.7

commit v5 on v4

--- a/solution.py
+++ b/solution.py
@@ -22,12 +22,15 @@
     return lax.shift_right_logical(count + (BLOCK - 1), 7)
 
 
-def pack_kernel(rank_ref, count_ref, obs_ref, state_ref, innov_ref, prec_ref,
+def pack_kernel(count_hbm, obs_ref, state_ref, innov_ref, prec_ref,
                 out_ref, weight_ref, push_ref,
-                innov_rows, prec_rows, line_ref, obs_sem, state_sem, innov_sem, prec_sem):
+                count_ref, innov_rows, prec_rows, line_ref,
+                count_sem, obs_sem, state_sem, innov_sem, prec_sem):
     pairs = out_ref.shape[0]
     slots = LIVE * BLOCK
-    rank = rank_ref[0]
+    rank = lax.axis_index("member")
+    count_copy = pltpu.make_async_copy(count_hbm, count_ref, count_sem)
+    count_copy.start()
     eight = pl.ds(pl.multiple_of(8 * lax.div(rank, 4), 8), 8)
     copies = [
         pltpu.make_async_copy(state_ref, out_ref.at[:, LIVE:], state_sem),
@@ -36,6 +39,7 @@
     ]
     for copy in copies:
         copy.start()
+    count_copy.wait()
 
     def start(pair, carry):
         first = blocks_used(count_ref[2 * pair])
@@ -72,14 +76,14 @@
     copies[0].wait()
 
 
-def pack(rank, obs_count, ens_obs, ens_state, innovation, obs_precision):
+def pack(obs_count, ens_obs, ens_state, innovation, obs_precision):
     tiles, members, slots = ens_obs.shape
     width = ens_state.shape[2]
     pairs = tiles // 2
     blocks = lambda x, n: x.reshape(tiles, members, n, BLOCK).transpose(0, 2, 1, 3)
     obs = blocks(ens_obs, slots // BLOCK)
     state = blocks(ens_state, width // BLOCK).reshape(pairs, 2 * width // BLOCK, members, BLOCK)
-    smem, hbm, vmem = (pl.BlockSpec(memory_space=m) for m in (pltpu.SMEM, pl.ANY, pltpu.VMEM))
+    hbm, vmem = (pl.BlockSpec(memory_space=m) for m in (pl.ANY, pltpu.VMEM))
     return pl.pallas_call(
         pack_kernel,
         out_shape=(
@@ -87,15 +91,16 @@
             pltpu.VMEM((8, slots), F32),
             pltpu.VMEM((16, slots), BF16),
         ),
-        in_specs=[smem, smem, hbm, hbm, hbm, hbm],
+        in_specs=[hbm] * 5,
         out_specs=(vmem, vmem, vmem),
         scratch_shapes=[
+            pltpu.SMEM((tiles,), jnp.int32),
             pltpu.VMEM((8, slots), F32),
             pltpu.VMEM((8, slots), F32),
             pltpu.VMEM((8, 2 * slots), F32),
-        ] + [pltpu.SemaphoreType.DMA] * 4,
+        ] + [pltpu.SemaphoreType.DMA] * 5,
         name="pack",
-    )(rank, obs_count, obs, state, innovation, obs_precision)
+    )(obs_count, obs, state, innovation, obs_precision)
 
 
 def mm(a, b):
@@ -213,10 +218,8 @@
 
 def local(ens_obs, ens_state, innovation, obs_precision, obs_count):
     tiles, each, variables = ens_state.shape
-    rank = lax.axis_index("member").astype(jnp.int32).reshape(1)
     exchange = lambda x: lax.all_to_all(x, "member", split_axis=0, concat_axis=0, tiled=True)
-    packed, weights, pushes = pack(
-        rank, obs_count, ens_obs, ens_state, innovation, obs_precision)
+    packed, weights, pushes = pack(obs_count, ens_obs, ens_state, innovation, obs_precision)
     back = exchange(analyse(exchange(packed), weights, pushes))
     back = back.reshape(tiles, variables // BLOCK, each, BLOCK)
     return back.transpose(0, 2, 1, 3).reshape(tiles, each, variables)

time: 86.5 us -> 86.4 us (level)
  the two profiles are of different devices: /device:TPU:18 before, /device:TPU:114 now
where the time goes in v5:
time: 86.4 us; the launch traced here: 86.2 us
  blocking collectives  80.9 us (94%)
  Pallas kernels  4.46 us (5%)
    all_to_all x2, blocking collectives, local(): lax.all_to_all(x, 'member', split_axis=0, concat_axis=0, tiled=True)  80.9 us
    pallas_call x1, Pallas kernels, analyse(): pl.pallas_call(analyse_kernel, out_shape=pltpu.VMEM((sources, blocks - LI...  2.46 us
    pallas_call x1, Pallas kernels, pack(): pl.pallas_call(pack_kernel, out_shape=(pltpu.VMEM((pairs, LIVE + state.sh...  1.99 us

profile of v5, /device:TPU:114, one launch (start us, length us, event | category | flops | bytes accessed | tf_op | source)
XLA Modules:
  0.0 86.2 jit_solution(1250233893693975882)
XLA Ops:
  0.0 2.0 %pack.1 = (bf16[32,24,8,128]{3,2,1,0:T(8,128)(2,1)S(1)}, f32[8,2048]{1,0:T(8,128)S(1)}, bf16[16,2048]{1,0:T(8,128)(2,1)S(1)}) custom-call(s32[64]{0:T(128)} %count_hbm.1, bf16[64,16,8,128]{3,2,1,0:T(8,128)(2,1)} %bitcast.13, bf16[32,8,8,128]{3,2,1,0:T(8,128)(2,1)} %bitcast.15, f32[64,2048]{1,0:T(8,128)} %innov_ref.1, f32[64,2048]{1,0:T(8,128)} %prec_ref.1), custom_call_target="tpu_custom_call" | custom-call | tf_op jit(solution)/shard_map/pack/pallas_call | solution.py:87
  2.0 59.0 %all_to_all.10.got_ref = bf16[32,24,8,128]{3,2,1,0:T(8,128)(2,1)S(1)} all-to-all(bf16[32,24,8,128]{3,2,1,0:T(8,128)(2,1)S(1)} %get-tuple-element.8), channel_id=1, replica_groups=mesh['region'=32,'member'=32] {'member'}, dimensions={0} | all-to-all | bytes 3145728 | tf_op jit(solution)/shard_map/all_to_all | solution.py:221
  61.0 2.5 %analyse.1 = bf16[32,8,8,128]{3,2,1,0:T(8,128)(2,1)S(1)} custom-call(bf16[32,24,8,128]{3,2,1,0:T(8,128)(2,1)S(1)} %all_to_all.10.got_ref, f32[8,2048]{1,0:T(8,128)S(1)} %get-tuple-element.9.weight_ref, bf16[16,2048]{1,0:T(8,128)(2,1)S(1)} %get-tuple-element.10.push_ref), custom_call_target="tpu_custom_call" | custom-call | tf_op jit(solution)/shard_map/analyse/pallas_call | solution.py:209
  63.5 21.9 %all_to_all.11 = bf16[32,8,8,128]{3,2,1,0:T(8,128)(2,1)S(1)} all-to-all(bf16[32,8,8,128]{3,2,1,0:T(8,128)(2,1)S(1)} %analyse.1), channel_id=1, replica_groups=mesh['region'=32,'member'=32] {'member'}, dimensions={0} | all-to-all | bytes 1048576 | tf_op jit(solution)/shard_map/all_to_all | solution.py:221
  85.4 0.8 copy.7
